TPU v7x, 32 devices: a whole 2x2x4 slice. The times are simulated.
32 devices in a mesh: dp: 4 (over x, core), blk: 8 (over z, y).
Axes of the slice: x: 2, y: 2, z: 4, core: 2. Of those that a mesh axis runs over, the one named last changes fastest.
Arguments:
- hidden_in: bfloat16 [2048, 8, 1024], P('blk', 'dp'), may hold values from -6 to 6
- first_values: bfloat16 [2048, 8, 1024], P('blk', 'dp'), may hold values from -13 to 13
- doc_lengths: int32 [8, 8], P('dp'), may hold values from 1 to 1024, 2048 in all within a row
- w_query: bfloat16 [1024, 1024], replicated, may hold values from -0.25 to 0.25
- w_key: bfloat16 [1024, 1024], replicated, may hold values from -0.25 to 0.25
- w_value: bfloat16 [1024, 1024], replicated, may hold values from -0.1875 to 0.1875
- w_out: bfloat16 [1024, 1024], replicated, may hold values from -0.75 to 0.75
- w_gate: bfloat16 [1024, 2816], replicated, may hold values from -0.1875 to 0.1875
- w_up: bfloat16 [1024, 2816], replicated, may hold values from -0.1875 to 0.1875
- w_down: bfloat16 [2816, 1024], replicated, may hold values from -0.109375 to 0.109375
- attn_gain: float32 [1024], replicated, may hold values from 0.5 to 1.5
- ffn_gain: float32 [1024], replicated, may hold values from 0.5 to 1.5
- out_cotangent: bfloat16 [2048, 8, 1024], P('blk', 'dp'), may hold values from -6 to 6
Outputs:
- block_out: bfloat16 [2048, 8, 1024], P('blk', 'dp')
- grad_input: float32 [2048, 8, 1024], P('blk', 'dp')
- grad_first: float32 [2048, 8, 1024], P('blk', 'dp')
- grad_query: float32 [1024, 1024], P('dp', 'blk')
- grad_key: float32 [1024, 1024], P('dp', 'blk')
- grad_value: float32 [1024, 1024], P('dp', 'blk')
- grad_project: float32 [1024, 1024], P('dp', 'blk')
- grad_gate: float32 [1024, 2816], P('dp', 'blk')
- grad_up: float32 [1024, 2816], P('dp', 'blk')
- grad_down: float32 [2816, 1024], P('dp', 'blk')
- grad_attn_gain: float32 [1024], replicated
- grad_ffn_gain: float32 [1024], replicated
- first_msq: float32 [], replicated
- mixed_msq: float32 [], replicated
Inputs may be any that keep to these rules, and one draw needn't show every extreme that they name: `doc_lengths`: the 8 lengths of a row sum to 2048.
All inputs are finite; a program needn't handle non-finite values.
Results may differ from a plain program's by a relative error of at most 0.033.
Values may be sent and summed in bfloat16 or wider, within the bound.
A program may use at most 320 MiB of HBM per device.

v0:
```python
import jax
import jax.numpy as jnp
from jax import lax
from jax.sharding import PartitionSpec as P

HEADS = 16
HEAD_DIM = 64
epsilon = 1e-06


def documents(doc_lengths, row_length):
    doc_ends = jnp.cumsum(doc_lengths, axis=1)
    places = jnp.arange(row_length, dtype=jnp.int32)
    passed = (doc_ends[:, None, :] <= places[None, :, None]).astype(jnp.int32)
    segment = jnp.sum(passed, axis=2)
    doc_start = jnp.sum(passed * doc_lengths[:, None, :], axis=2)
    return (segment, places[None, :] - doc_start)


def project(acts, weight):
    flat = acts.reshape(-1, acts.shape[-1])
    result = jnp.dot(flat, weight, preferred_element_type=jnp.float32)
    return result.reshape(acts.shape[:-1] + (weight.shape[1],))


def project_back(grads_in, weight):
    flat = grads_in.reshape(-1, grads_in.shape[-1])
    result = lax.dot_general(
        flat, weight, (((1,), (1,)), ((), ())), preferred_element_type=jnp.float32
    )
    return result.reshape(grads_in.shape[:-1] + (weight.shape[0],))


def weight_grad(acts, grads_in):
    flat_acts = acts.reshape(-1, acts.shape[-1])
    flat_grads = grads_in.reshape(-1, grads_in.shape[-1])
    return lax.dot_general(
        flat_acts, flat_grads, (((0,), (0,)), ((), ())), preferred_element_type=jnp.float32
    )


def rms_parts(values):
    inverse_rms = lax.rsqrt(jnp.mean(values * values, axis=-1, keepdims=True) + epsilon)
    return (values * inverse_rms, inverse_rms)


def norm_back(d_normed, normed, inverse_rms):
    return inverse_rms * (d_normed - normed * jnp.mean(d_normed * normed, axis=-1, keepdims=True))


def rope_tables(positions):
    half_dim = HEAD_DIM // 2
    inverse_freq = jnp.power(10000.0, -jnp.arange(half_dim, dtype=jnp.float32) * 2.0 / HEAD_DIM)
    angles = jnp.transpose(positions).astype(jnp.float32)[:, :, None] * inverse_freq[None, None, :]
    return (jnp.cos(angles)[:, :, None, :], jnp.sin(angles)[:, :, None, :])


def rotate(values, cos_table, sin_table):
    half_dim = HEAD_DIM // 2
    shaped = values.reshape(values.shape[:-1] + (HEADS, HEAD_DIM))
    first_half = shaped[..., :half_dim]
    second_half = shaped[..., half_dim:]
    turned = jnp.concatenate(
        [
            first_half * cos_table - second_half * sin_table,
            second_half * cos_table + first_half * sin_table,
        ],
        axis=-1,
    )
    return turned.reshape(values.shape)


def body(
    hidden_in,
    first_values,
    doc_lengths,
    w_query,
    w_key,
    w_value,
    w_out,
    w_gate,
    w_up,
    w_down,
    attn_gain,
    ffn_gain,
    out_cotangent,
):
    local_len, seq_count, model_width = hidden_in.shape
    cycle_size = lax.axis_size("blk")
    row_length = local_len * cycle_size
    offset = lax.axis_index("blk") * local_len
    score_scale = HEAD_DIM ** (-0.5)
    segment_all, position_all = documents(doc_lengths, row_length)
    segment_own = lax.dynamic_slice_in_dim(segment_all, offset, local_len, 1)
    position_own = lax.dynamic_slice_in_dim(position_all, offset, local_len, 1)
    query_index = offset + jnp.arange(local_len, dtype=jnp.int32)
    cos_table, sin_table = rope_tables(position_own)
    resid_in = hidden_in.astype(jnp.float32)
    normed_one, inv_one = rms_parts(resid_in)
    normed_in = (normed_one * attn_gain).astype(jnp.bfloat16)
    queries = rotate(project(normed_in, w_query), cos_table, sin_table).astype(jnp.bfloat16)
    keys_rot = rotate(project(normed_in, w_key), cos_table, sin_table).astype(jnp.bfloat16)
    first_f = first_values.astype(jnp.float32)
    mixed = 0.5 * project(normed_in, w_value) + 0.5 * first_f
    mixed_low = mixed.astype(jnp.bfloat16)
    first_sq = jnp.sum(first_f * first_f)
    mixed_sq = jnp.sum(mixed * mixed)
    query_four = queries.reshape(local_len, seq_count, HEADS, HEAD_DIM)

    def allowed_pairs(start, n_keys):
        key_index = start + jnp.arange(n_keys, dtype=jnp.int32)
        segment_key = lax.dynamic_slice_in_dim(segment_all, start, n_keys, 1)
        allowed = (key_index[None, None, :] <= query_index[None, :, None]) & (
            segment_key[:, None, :] == segment_own[:, :, None]
        )
        return allowed[:, None]

    def piece_step(running, key_piece, value_piece, start):
        run_max, run_sum, run_acc = running
        n_keys = key_piece.shape[0]
        allowed = allowed_pairs(start, n_keys)
        key_four = key_piece.reshape(n_keys, seq_count, HEADS, HEAD_DIM)
        value_four = value_piece.reshape(n_keys, seq_count, HEADS, HEAD_DIM)
        scores = (
            jnp.einsum("qshd,kshd->shqk", query_four, key_four, preferred_element_type=jnp.float32)
            * score_scale
        )
        new_max = jnp.maximum(run_max, jnp.max(jnp.where(allowed, scores, -1e30), axis=-1))
        weights = jnp.where(allowed, jnp.exp(scores - new_max[..., None]), 0.0)
        factor = jnp.exp(run_max - new_max)
        run_sum = run_sum * factor + jnp.sum(weights, axis=-1)
        run_acc = run_acc * factor[..., None] + jnp.einsum(
            "shqk,kshd->shqd",
            weights.astype(jnp.bfloat16),
            value_four,
            preferred_element_type=jnp.float32,
        )
        return (new_max, run_sum, run_acc)

    start_state = (
        jnp.full((seq_count, HEADS, local_len), -1e30, jnp.float32),
        jnp.zeros((seq_count, HEADS, local_len), jnp.float32),
        jnp.zeros((seq_count, HEADS, local_len, HEAD_DIM), jnp.float32),
    )
    running = start_state
    key_piece = lax.all_gather(keys_rot, "blk", axis=0, tiled=True)
    value_piece = lax.all_gather(mixed_low, "blk", axis=0, tiled=True)
    n_keys = key_piece.shape[0]
    step_rows = min(512, n_keys)
    n_steps = n_keys // step_rows

    def inner_step(fold_state, block_item):
        return (piece_step(fold_state, block_item[0], block_item[1], block_item[2]), None)

    starts = jnp.arange(n_steps, dtype=jnp.int32) * step_rows
    running, unused = lax.scan(
        inner_step,
        running,
        (
            key_piece.reshape(n_steps, step_rows, seq_count, model_width),
            value_piece.reshape(n_steps, step_rows, seq_count, model_width),
            starts,
        ),
    )
    run_max, run_sum, run_acc = running
    attn_four = jnp.transpose(run_acc / run_sum[..., None], (2, 0, 1, 3))
    attn_f = attn_four.reshape(local_len, seq_count, model_width)
    log_total = run_max + jnp.log(run_sum)
    attn_low = attn_f.astype(jnp.bfloat16)
    resid_mid = resid_in + project(attn_low, w_out)
    normed_two, inv_two = rms_parts(resid_mid)
    normed_mid = (normed_two * ffn_gain).astype(jnp.bfloat16)
    gate_pre = project(normed_mid, w_gate)
    up_pre = project(normed_mid, w_up)
    gate_act = jax.nn.silu(gate_pre)
    inner_low = (gate_act * up_pre).astype(jnp.bfloat16)
    block_out = (resid_mid + project(inner_low, w_down)).astype(jnp.bfloat16)
    grad_down = weight_grad(inner_low, out_cotangent)
    d_inner = project_back(out_cotangent, w_down)
    sigmoid_gate = jax.nn.sigmoid(gate_pre)
    d_gate = (d_inner * up_pre * sigmoid_gate * (1.0 + gate_pre * (1.0 - sigmoid_gate))).astype(
        jnp.bfloat16
    )
    d_up = (d_inner * gate_act).astype(jnp.bfloat16)
    grad_gate = weight_grad(normed_mid, d_gate)
    grad_up = weight_grad(normed_mid, d_up)
    d_normed_mid = project_back(d_gate, w_gate) + project_back(d_up, w_up)
    gain_two_grad = jnp.sum((d_normed_mid * normed_two).reshape(-1, model_width), axis=0)
    d_resid_mid = out_cotangent.astype(jnp.float32) + norm_back(
        d_normed_mid * ffn_gain, normed_two, inv_two
    )
    d_branch = d_resid_mid.astype(jnp.bfloat16)
    grad_project = weight_grad(attn_low, d_branch)
    d_attn = project_back(d_branch, w_out).astype(jnp.bfloat16)
    d_attn_four = d_attn.reshape(local_len, seq_count, HEADS, HEAD_DIM)
    delta_rows = jnp.transpose(
        jnp.sum(d_attn_four.astype(jnp.float32) * attn_four, axis=-1), (1, 2, 0)
    )
    back_keys, back_values = (
        lax.all_gather(keys_rot, "blk", axis=0, tiled=True),
        lax.all_gather(mixed_low, "blk", axis=0, tiled=True),
    )
    block_rows = min(512, row_length)
    n_blocks = row_length // block_rows
    block_starts = jnp.arange(n_blocks, dtype=jnp.int32) * block_rows

    def block_scores(key_four, value_four, start):
        allowed = allowed_pairs(start, block_rows)
        scores = (
            jnp.einsum("qshd,kshd->shqk", query_four, key_four, preferred_element_type=jnp.float32)
            * score_scale
        )
        probs = jnp.where(allowed, jnp.exp(scores - log_total[..., None]), 0.0)
        d_probs = jnp.einsum(
            "qshd,kshd->shqk", d_attn_four, value_four, preferred_element_type=jnp.float32
        )
        d_scores = (probs * (d_probs - delta_rows[..., None])).astype(jnp.bfloat16)
        return (probs, d_scores)

    def back_step(d_query_acc, block_item):
        key_block, value_block, start = block_item
        key_four = key_block.reshape(block_rows, seq_count, HEADS, HEAD_DIM)
        value_four = value_block.reshape(block_rows, seq_count, HEADS, HEAD_DIM)
        probs, d_scores = block_scores(key_four, value_four, start)
        d_query_acc = (
            d_query_acc
            + jnp.einsum("shqk,kshd->qshd", d_scores, key_four, preferred_element_type=jnp.float32)
            * score_scale
        )
        d_keys = (
            jnp.einsum("shqk,qshd->kshd", d_scores, query_four, preferred_element_type=jnp.float32)
            * score_scale
        )
        d_vals = jnp.einsum(
            "shqk,qshd->kshd",
            probs.astype(jnp.bfloat16),
            d_attn_four,
            preferred_element_type=jnp.float32,
        )
        joined = jnp.concatenate(
            [
                d_keys.reshape(block_rows, seq_count, model_width),
                d_vals.reshape(block_rows, seq_count, model_width),
            ],
            axis=-1,
        )
        return (d_query_acc, joined)

    d_query_rot, terms = lax.scan(
        back_step,
        jnp.zeros((local_len, seq_count, HEADS, HEAD_DIM), jnp.float32),
        (
            back_keys.reshape(n_blocks, block_rows, seq_count, model_width),
            back_values.reshape(n_blocks, block_rows, seq_count, model_width),
            block_starts,
        ),
    )
    terms = terms.reshape(row_length, seq_count, 2 * model_width)
    kv_grad = lax.psum_scatter(
        terms.astype(jnp.bfloat16), "blk", scatter_dimension=0, tiled=True
    ).astype(jnp.float32)
    d_key_rot = kv_grad[..., :model_width]
    d_mixed = kv_grad[..., model_width:]
    d_query_low = rotate(
        d_query_rot.reshape(local_len, seq_count, model_width), cos_table, -sin_table
    ).astype(jnp.bfloat16)
    d_key_low = rotate(d_key_rot, cos_table, -sin_table).astype(jnp.bfloat16)
    d_value_low = (0.5 * d_mixed).astype(jnp.bfloat16)
    grad_first = 0.5 * d_mixed
    grad_query = weight_grad(normed_in, d_query_low)
    grad_key = weight_grad(normed_in, d_key_low)
    grad_value = weight_grad(normed_in, d_value_low)
    d_normed_in = (
        project_back(d_query_low, w_query)
        + project_back(d_key_low, w_key)
        + project_back(d_value_low, w_value)
    )
    gain_one_grad = jnp.sum((d_normed_in * normed_one).reshape(-1, model_width), axis=0)
    grad_input = d_resid_mid + norm_back(d_normed_in * attn_gain, normed_one, inv_one)
    weight_grads = (grad_query, grad_key, grad_value, grad_project, grad_gate, grad_up, grad_down)
    partial_grads = (
        lax.psum_scatter(
            weight_grads[0].astype(jnp.bfloat16), "dp", scatter_dimension=0, tiled=True
        ).astype(jnp.float32),
        lax.psum_scatter(
            weight_grads[1].astype(jnp.bfloat16), "dp", scatter_dimension=0, tiled=True
        ).astype(jnp.float32),
        lax.psum_scatter(
            weight_grads[2].astype(jnp.bfloat16), "dp", scatter_dimension=0, tiled=True
        ).astype(jnp.float32),
        lax.psum_scatter(
            weight_grads[3].astype(jnp.bfloat16), "dp", scatter_dimension=0, tiled=True
        ).astype(jnp.float32),
        lax.psum_scatter(
            weight_grads[4].astype(jnp.bfloat16), "dp", scatter_dimension=0, tiled=True
        ).astype(jnp.float32),
        lax.psum_scatter(
            weight_grads[5].astype(jnp.bfloat16), "dp", scatter_dimension=0, tiled=True
        ).astype(jnp.float32),
        lax.psum_scatter(
            weight_grads[6].astype(jnp.bfloat16), "dp", scatter_dimension=0, tiled=True
        ).astype(jnp.float32),
    )
    summed = (
        lax.psum_scatter(
            partial_grads[0].astype(jnp.bfloat16), "blk", scatter_dimension=1, tiled=True
        ).astype(jnp.float32),
        lax.psum_scatter(
            partial_grads[1].astype(jnp.bfloat16), "blk", scatter_dimension=1, tiled=True
        ).astype(jnp.float32),
        lax.psum_scatter(
            partial_grads[2].astype(jnp.bfloat16), "blk", scatter_dimension=1, tiled=True
        ).astype(jnp.float32),
        lax.psum_scatter(
            partial_grads[3].astype(jnp.bfloat16), "blk", scatter_dimension=1, tiled=True
        ).astype(jnp.float32),
        lax.psum_scatter(
            partial_grads[4].astype(jnp.bfloat16), "blk", scatter_dimension=1, tiled=True
        ).astype(jnp.float32),
        lax.psum_scatter(
            partial_grads[5].astype(jnp.bfloat16), "blk", scatter_dimension=1, tiled=True
        ).astype(jnp.float32),
        lax.psum_scatter(
            partial_grads[6].astype(jnp.bfloat16), "blk", scatter_dimension=1, tiled=True
        ).astype(jnp.float32),
    )
    totals = lax.psum((gain_one_grad, gain_two_grad, first_sq, mixed_sq), ("dp", "blk"))
    n_entries = row_length * seq_count * lax.axis_size("dp") * model_width
    return (
        block_out,
        grad_input,
        grad_first,
        summed[0],
        summed[1],
        summed[2],
        summed[3],
        summed[4],
        summed[5],
        summed[6],
        totals[0],
        totals[1],
        totals[2] / n_entries,
        totals[3] / n_entries,
    )


def solution(mesh):
    in_specs = (
        P("blk", "dp", None),
        P("blk", "dp", None),
        P("dp", None),
        P(),
        P(),
        P(),
        P(),
        P(),
        P(),
        P(),
        P(),
        P(),
        P("blk", "dp", None),
    )
    out_specs = (
        P("blk", "dp", None),
        P("blk", "dp", None),
        P("blk", "dp", None),
        P("dp", "blk"),
        P("dp", "blk"),
        P("dp", "blk"),
        P("dp", "blk"),
        P("dp", "blk"),
        P("dp", "blk"),
        P("dp", "blk"),
        P(),
        P(),
        P(),
        P(),
    )
    return jax.shard_map(body, mesh=mesh, in_specs=in_specs, out_specs=out_specs, check_vma=False)
```

profile of v0, /device:TPU:0, one launch (start us, length us, event | category | flops | bytes accessed | tf_op | source)
XLA Modules:
  0.0 1740.5 jit_solution(13050748668814698923)
XLA Ops:
  42.2 99.5 %all-gather.5.cloned.1.call-done = bf16[2048,2,1024]{2,0,1:T(8,128)(2,1)} async-done(((bf16[256,2,1024]{2,0,1:T(8,128)(2,1)}), bf16[2048,2,1024]{2,0,1:T(8,128)(2,1)}) %all-gather.5.cloned.1.call-update) | async-done | bytes 8388624 | tf_op jit(solution)/shard_map/all_gather | solution.py:147
  141.7 11.7 copy.140
  153.4 114.2 %all-gather.3.cloned.1.call-done = bf16[2048,2,1024]{2,0,1:T(8,128)(2,1)} async-done(((bf16[256,2,1024]{2,0,1:T(8,128)(2,1)}), bf16[2048,2,1024]{2,0,1:T(8,128)(2,1)}) %all-gather.3.cloned.1.call-update) | async-done | bytes 8388624 | tf_op jit(solution)/shard_map/all_gather | solution.py:146
  267.6 11.5 copy.139
  279.1 144.7 %while.28 = (s32[]{:T(128)}, f32[2,16,256]{2,1,0:T(8,128)S(1)}, f32[2,16,256]{2,1,0:T(8,128)S(1)}, f32[2,16,256,64]{2,3,1,0:T(8,128)}, s32[4]{0:T(128)S(1)}, /*i...) while((s32[]{:T(128)}, f32[2,16,256]{2,1,0:T(8,128)S(1)}, ...), condition=%wide.region_7.8_spmd.clone, body=%wide.region_4.0_spmd.clone.sunk | while | flops 1122149120 | bytes 70013144 | solution.py:156
  303.7 11.1 fusion.161
  339.4 11.7 fusion.161
  375.7 11.7 fusion.161
  412.0 11.7 fusion.161
  436.6 10.4 multiply_convert_fusion.1
  465.8 192.9 %while.29 = (s32[]{:T(128)}, f32[256,2,16,64]{0,3,2,1:T(8,128)}, bf16[4,512,2,2048]{1,3,2,0:T(8,128)(2,1)}, bf16[4,512,2,1024]{1,3,2,0:T(8,128)(2,1)}, s32[4]{0:...) while((s32[]{:T(128)}, f32[256,2,16,64]{0,3,2,1:T(8,128)}, ...), condition=%wide.region_12.13_spmd.clone, body=%wide.region_11.12_spmd.clone.sunk | while | flops 2739012352 | bytes 129093912 | solution.py:249
  483.7 10.6 fusion.174
  530.7 10.6 fusion.174
  579.3 10.6 fusion.174
  627.8 10.6 fusion.174
  658.7 21.6 %copy.148 = bf16[4,512,2,2048]{3,1,0,2:T(8,128)(2,1)} copy(bf16[4,512,2,2048]{1,3,2,0:T(8,128)(2,1)} %get-tuple-element.145) | data formatting | bytes 33554432 | tf_op jit(solution)/shard_map/convert_element_type | solution.py:260
  709.0 251.6 %reduce-scatter.30.cloned.1.call-done = bf16[256,2,2048]{2,0,1:T(8,128)(2,1)} async-done(((bf16[2048,2,2048]{2,0,1:T(8,128)(2,1)}), bf16[256,2,2048]{2,0,1:T(8,128)(2,1)}) %reduce-scatter.30.cloned.1.call-update) | async-done | bytes 2097168 | tf_op jit(solution)/shard_map/reduce_scatter | solution.py:259
  967.9 26.4 %reduce-scatter.38.cloned.1.call-done = bf16[256,1024]{1,0:T(8,128)(2,1)} async-done(((bf16[1024,1024]{1,0:T(8,128)(2,1)}), bf16[256,1024]{1,0:T(8,128)(2,1)}) %reduce-scatter.38.cloned.1.call-update) | async-done | bytes 524304 | tf_op jit(solution)/shard_map/reduce_scatter | solution.py:291
  996.4 55.2 %reduce-scatter.40.cloned.1.call-done = bf16[256,2816]{1,0:T(8,128)(2,1)} async-done(((bf16[1024,2816]{1,0:T(8,128)(2,1)}), bf16[256,2816]{1,0:T(8,128)(2,1)}) %reduce-scatter.40.cloned.1.call-update) | async-done | bytes 1441808 | tf_op jit(solution)/shard_map/reduce_scatter | solution.py:294
  1054.2 54.8 %reduce-scatter.42.cloned.1.call-done = bf16[256,2816]{1,0:T(8,128)(2,1)} async-done(((bf16[1024,2816]{1,0:T(8,128)(2,1)}), bf16[256,2816]{1,0:T(8,128)(2,1)}) %reduce-scatter.42.cloned.1.call-update) | async-done | bytes 1441808 | tf_op jit(solution)/shard_map/reduce_scatter | solution.py:297
  1111.7 54.8 %reduce-scatter.44.cloned.1.call-done = bf16[704,1024]{1,0:T(8,128)(2,1)} async-done(((bf16[2816,1024]{1,0:T(8,128)(2,1)}), bf16[704,1024]{1,0:T(8,128)(2,1)}) %reduce-scatter.44.cloned.1.call-update) | async-done | bytes 1441808 | tf_op jit(solution)/shard_map/reduce_scatter | solution.py:300
  1187.5 13.2 reduce-scatter.36.cloned.1.call-done
  1214.4 51.5 %reduce-scatter.52.cloned.1.call-done = bf16[128,256]{1,0:T(8,128)(2,1)} async-done(((bf16[1024,256]{1,0:T(8,128)(2,1)}), bf16[128,256]{1,0:T(8,128)(2,1)}) %reduce-scatter.52.cloned.1.call-update) | async-done | bytes 65552
  1267.6 66.0 %reduce-scatter.54.cloned.1.call-done = bf16[352,256]{1,0:T(8,128)(2,1)} async-done(((bf16[2816,256]{1,0:T(8,128)(2,1)}), bf16[352,256]{1,0:T(8,128)(2,1)}) %reduce-scatter.54.cloned.1.call-update) | async-done | bytes 180240
  1335.5 65.7 %reduce-scatter.56.cloned.1.call-done = bf16[352,256]{1,0:T(8,128)(2,1)} async-done(((bf16[2816,256]{1,0:T(8,128)(2,1)}), bf16[352,256]{1,0:T(8,128)(2,1)}) %reduce-scatter.56.cloned.1.call-update) | async-done | bytes 180240
  1403.2 65.4 %reduce-scatter.58.cloned.1.call-done = bf16[128,704]{1,0:T(8,128)(2,1)} async-done(((bf16[1024,704]{1,0:T(8,128)(2,1)}), bf16[128,704]{1,0:T(8,128)(2,1)}) %reduce-scatter.58.cloned.1.call-update) | async-done | bytes 180240
  1470.5 31.6 %reduce-scatter.34.cloned.1.call-done = bf16[256,1024]{1,0:T(8,128)(2,1)} async-done(((bf16[1024,1024]{1,0:T(8,128)(2,1)}), bf16[256,1024]{1,0:T(8,128)(2,1)}) %reduce-scatter.34.cloned.1.call-update) | async-done | bytes 524304 | tf_op jit(solution)/shard_map/reduce_scatter | solution.py:285
  1514.2 21.9 %reduce-scatter.32.cloned.1.call-done = bf16[256,1024]{1,0:T(8,128)(2,1)} async-done(((bf16[1024,1024]{1,0:T(8,128)(2,1)}), bf16[256,1024]{1,0:T(8,128)(2,1)}) %reduce-scatter.32.cloned.1.call-update) | async-done | bytes 524304 | tf_op jit(solution)/shard_map/reduce_scatter | solution.py:282
  1544.2 39.7 %all-reduce = (f32[1024]{0:T(1024)}, f32[1024]{0:T(1024)}, f32[]{:T(128)}, f32[]{:T(128)}) all-reduce(f32[1024]{0:T(1024)S(1)} %get-tuple-element.384, f32[1024]{0:T(1024)S(1)} %copy-done.32, f32[]{:T(128)} %fusion.47, f32[]{:T(128)} %get-tuple-element.459), channel_id=1, replica_groups=mesh['dp'=4,'blk'=8] {'dp','blk'}, use_global_device_ids=true, to_apply=%region_30.31 | all-reduce | flops 2050 | bytes 16400 | tf_op jit(solution)/shard_map/psum | solution.py:327
  1590.9 10.4 reduce-scatter.50.cloned.1.call-done
  1602.9 62.8 %reduce-scatter.48.cloned.1.call-done = bf16[128,256]{1,0:T(8,128)(2,1)} async-done(((bf16[1024,256]{1,0:T(8,128)(2,1)}), bf16[128,256]{1,0:T(8,128)(2,1)}) %reduce-scatter.48.cloned.1.call-update) | async-done | bytes 65552
  1667.3 62.6 %reduce-scatter.46.cloned.1.call-done = bf16[128,256]{1,0:T(8,128)(2,1)} async-done(((bf16[1024,256]{1,0:T(8,128)(2,1)}), bf16[128,256]{1,0:T(8,128)(2,1)}) %reduce-scatter.46.cloned.1.call-update) | async-done | bytes 65552
  (301 shorter events, 415.0 us)
Async XLA Ops:
  7.2 134.5 %all-gather.5.cloned.1.call-start = ((), (), s32[]{:S(2)}) async-start(), calls=%async_computation.16 | async-start | bytes 9437184 | tf_op jit(solution)/shard_map/all_gather | solution.py:147
  9.1 18.2 %copy-start.28 = (f32[256,2]{0,1:T(2,128)}, f32[256,2]{0,1:T(2,128)S(1)}, u32[]{:S(2)}) copy-start(f32[256,2]{0,1:T(2,128)S(1)} %add_rsqrt_fusion.1) | copy-start | bytes 6148
  13.9 253.7 %all-gather.3.cloned.1.call-start = ((), (), s32[]{:S(2)}) async-start(), calls=%async_computation.15 | async-start | bytes 9437184 | tf_op jit(solution)/shard_map/all_gather | solution.py:146
  31.8 928.8 %reduce-scatter.30.cloned.1.call-start = ((), (), s32[]{:S(2)}) async-start(), calls=%async_computation.17 | async-start | bytes 18874368 | tf_op jit(solution)/shard_map/reduce_scatter | solution.py:259
  426.4 10.2 slice-start.2
  427.8 29.2 %copy-start.3 = (f32[256,2,1024]{2,0,1:T(8,128)}, f32[256,2,1024]{2,0,1:T(8,128)S(1)}, u32[]{:S(2)}) copy-start(f32[256,2,1024]{2,0,1:T(8,128)S(1)} %get-tuple-element.470) | copy-start | bytes 6291460
  428.1 8.4 copy-start.15
  428.1 8.4 slice-start.3
  428.1 18.9 %slice-start = ((s8[5767168]{0:T(1024)(128)(4,1)}), s8[4194304]{0:T(1024)(128)(4,1)S(1)}, s32[]{:S(2)}) async-start(s8[5767168]{0:T(1024)(128)(4,1)} %bitcast.283), calls=%async_computation.32 | async-start | bytes 8388608
  436.6 10.4 slice-start.1
  447.0 6.0 copy-start.33
  494.2 9.4 copy-start.2
  541.3 9.4 copy-start.2
  589.9 9.4 copy-start.2
  638.4 9.4 copy-start.2
  680.4 313.9 %reduce-scatter.38.cloned.1.call-start = ((), (), s32[]{:S(2)}) async-start(), calls=%async_computation.21 | async-start | bytes 2621440 | tf_op jit(solution)/shard_map/reduce_scatter | solution.py:291
  685.8 365.8 %reduce-scatter.40.cloned.1.call-start = ((), (), s32[]{:S(2)}) async-start(), calls=%async_computation.22 | async-start | bytes 7208960 | tf_op jit(solution)/shard_map/reduce_scatter | solution.py:294
  693.9 415.1 %reduce-scatter.42.cloned.1.call-start = ((), (), s32[]{:S(2)}) async-start(), calls=%async_computation.23 | async-start | bytes 7208960 | tf_op jit(solution)/shard_map/reduce_scatter | solution.py:297
  700.8 465.7 %reduce-scatter.44.cloned.1.call-start = ((), (), s32[]{:S(2)}) async-start(), calls=%async_computation.24 | async-start | bytes 7208960 | tf_op jit(solution)/shard_map/reduce_scatter | solution.py:300
  709.0 255.9 %copy-start.7 = (bf16[256,2,1024]{2,1,0:T(2,128)(2,1)S(1)}, bf16[256,2,1024]{2,1,0:T(2,128)(2,1)}, u32[]{:S(2)}) copy-start(bf16[256,2,1024]{2,1,0:T(2,128)(2,1)} %param.17) | copy-start | bytes 3145732
  709.0 255.9 %copy-start.27 = (f32[1024]{0:T(1024)S(1)}, f32[1024]{0:T(1024)}, u32[]{:S(2)}) copy-start(f32[1024]{0:T(1024)} %param.27) | copy-start | bytes 12292
  709.0 255.9 %copy-start.29 = (f32[256,2]{0,1:T(2,128)S(1)}, f32[256,2]{0,1:T(2,128)}, u32[]{:S(2)}) copy-start(f32[256,2]{0,1:T(2,128)} %copy-done.28) | copy-start | bytes 6148
  709.0 491.7 %reduce-scatter.36.cloned.1.call-start = ((), (), s32[]{:S(2)}) async-start(), calls=%async_computation.20 | async-start | bytes 2621440 | tf_op jit(solution)/shard_map/reduce_scatter | solution.py:288
  967.8 298.1 %reduce-scatter.52.cloned.1.call-start = ((), (), s32[]{:S(2)}) async-start(), calls=%async_computation.28 | async-start | bytes 589824
  996.3 337.2 %reduce-scatter.54.cloned.1.call-start = ((), (), s32[]{:S(2)}) async-start(), calls=%async_computation.29 | async-start | bytes 1622016
  1054.2 347.0 %reduce-scatter.56.cloned.1.call-start = ((), (), s32[]{:S(2)}) async-start(), calls=%async_computation.30 | async-start | bytes 1622016
  1111.6 357.0 %reduce-scatter.58.cloned.1.call-start = ((), (), s32[]{:S(2)}) async-start(), calls=%async_computation.31 | async-start | bytes 1769472
  1169.1 333.0 %reduce-scatter.34.cloned.1.call-start = ((), (), s32[]{:S(2)}) async-start(), calls=%async_computation.19 | async-start | bytes 2621440 | tf_op jit(solution)/shard_map/reduce_scatter | solution.py:285
  1183.1 353.0 %reduce-scatter.32.cloned.1.call-start = ((), (), s32[]{:S(2)}) async-start(), calls=%async_computation.18 | async-start | bytes 2621440 | tf_op jit(solution)/shard_map/reduce_scatter | solution.py:282
  1187.4 413.8 %reduce-scatter.50.cloned.1.call-start = ((), (), s32[]{:S(2)}) async-start(), calls=%async_computation.27 | async-start | bytes 589824
  1202.7 463.0 %reduce-scatter.48.cloned.1.call-start = ((), (), s32[]{:S(2)}) async-start(), calls=%async_computation.26 | async-start | bytes 589824
  1504.1 225.8 %reduce-scatter.46.cloned.1.call-start = ((), (), s32[]{:S(2)}) async-start(), calls=%async_computation.25 | async-start | bytes 589824
  (29 other events, 77.4 us)
Sparse Core Ops, SparseCore 0:
  14.1 127.5 all-gather.4
  144.5 123.0 all-gather.2
  680.5 280.1 reduce-scatter.29
  963.8 30.4 reduce-scatter.37
  996.7 54.8 reduce-scatter.39
  1054.1 54.8 reduce-scatter.41
  1111.6 54.8 reduce-scatter.43
  1169.2 31.4 reduce-scatter.35
  1204.0 61.8 reduce-scatter.51
  1269.6 63.9 reduce-scatter.53
  1337.4 63.8 reduce-scatter.55
  1404.9 63.6 reduce-scatter.57
  1471.7 30.3 reduce-scatter.33
  1504.6 31.4 reduce-scatter.31
  1539.3 61.9 reduce-scatter.49
  1604.8 60.8 reduce-scatter.47
  1668.9 60.9 reduce-scatter.45
where the time goes:
time: 1750 us; the launch traced here: 1740 us
  waiting for transfers between devices  1110 us (63%)
  matrix products  317 us (18%)
  local copies, waits for them, and re-layouts  150 us (9%)
  other arithmetic  89.3 us (5%)
  blocking collectives  39.7 us (2%)
  between operations  18.2 us (1%)
    unnamed x24, waiting for transfers between devices  385 us
    reduce_scatter x1, waiting for transfers between devices, body(): lax.psum_scatter(terms.astype(jnp.bfloat16), 'blk', scatter_dimension=0,...  252 us
    all_gather x1, waiting for transfers between devices, body(): key_piece = lax.all_gather(keys_rot, 'blk', axis=0, tiled=True)  114 us
    all_gather x1, waiting for transfers between devices, body(): value_piece = lax.all_gather(mixed_low, 'blk', axis=0, tiled=True)  99.5 us
    unnamed x95, local copies, waits for them, and re-layouts  72 us
    reduce_scatter x1, waiting for transfers between devices, body(): lax.psum_scatter(weight_grads[4].astype(jnp.bfloat16), 'dp', scatter_dime...  55.2 us
    reduce_scatter x1, waiting for transfers between devices, body(): lax.psum_scatter(weight_grads[6].astype(jnp.bfloat16), 'dp', scatter_dime...  54.8 us
    reduce_scatter x1, waiting for transfers between devices, body(): lax.psum_scatter(weight_grads[5].astype(jnp.bfloat16), 'dp', scatter_dime...  54.8 us
  transfers between devices with their start and end apart: 17, of which 17 were waited for; matrix products, arithmetic and copies ran while one was open for 8% of the time, Pallas kernels for 0%

commit v1 on v0

--- a/solution.py
+++ b/solution.py
@@ -6,6 +6,12 @@
 HEADS = 16
 HEAD_DIM = 64
 epsilon = 1e-06
+
+
+def in_order(tiles, dim):
+    tiles = jnp.moveaxis(tiles, 0, dim)
+    dims = tiles.shape
+    return tiles.reshape(*dims[:dim], dims[dim] * dims[dim + 1], *dims[dim + 2 :])
 
 
 def documents(doc_lengths, row_length):
@@ -144,7 +150,19 @@
     )
     running = start_state
     key_piece = lax.all_gather(keys_rot, "blk", axis=0, tiled=True)
-    value_piece = lax.all_gather(mixed_low, "blk", axis=0, tiled=True)
+    size = lax.axis_size("blk")
+    pairs = [(i, (i + 1) % size) for i in range(size)]
+    back = [(b, a) for a, b in pairs]
+    lower, upper = ([], [])
+    for step in range(size - 1):
+        if step % 2 == 0:
+            lower.append(lax.ppermute(lower[-1] if lower else mixed_low, "blk", pairs))
+        else:
+            upper.append(lax.ppermute(upper[-1] if upper else mixed_low, "blk", back))
+    tiles = jnp.stack([*lower[::-1], mixed_low, *upper])
+    shift = lax.axis_index("blk") - len(lower)
+    tiles = tiles[(jnp.arange(size) - shift) % size]
+    value_piece = in_order(tiles, 0)
     n_keys = key_piece.shape[0]
     step_rows = min(512, n_keys)
     n_steps = n_keys // step_rows

time: 1750 us -> 1840 us (1.051)
  starting transfers between devices: 1.81 us -> 81.8 us
  local copies, waits for them, and re-layouts: 150 us -> 211 us
  waiting for transfers between devices: 1110 us -> 1050 us
    ppermute x0 -> x7, waiting for transfers between devices: none -> 139 us  [the longest x4 139 us: body(): lower.append(lax.ppermute(lower[-1] if lower else mixed_low, 'blk', pairs))]
    all_gather x1, waiting for transfers between devices: 114 us -> 0.01 us  [body(): key_piece = lax.all_gather(keys_rot, 'blk', axis=0, tiled=True)]
    all_gather x1, waiting for transfers between devices: 99.5 us -> 0.02 us  [body(): lax.all_gather(mixed_low, 'blk', axis=0, tiled=True)]
    ppermute x0 -> x7, starting transfers between devices: none -> 80.9 us  [the longest x3 72.8 us: body(): upper.append(lax.ppermute(upper[-1] if upper else mixed_low, 'blk', back))]
    dynamic_slice x16 -> x32, local copies, waits for them, and re-layouts: 35.2 us -> 74.7 us  [body(): lax.scan(inner_step, running, (key_piece.reshape(n_steps, step_rows, seq_...]
    unnamed x95 -> x109, local copies, waits for them, and re-layouts: 72 us -> 74.2 us
  transfers between devices with their start and end apart: 17 -> 24, of which waited for: 17 -> 19; matrix products, arithmetic and copies ran while one was open for 8% -> 20% of each run, Pallas kernels for 0% -> 0%
where the time goes in v1:
time: 1840 us; the launch traced here: 1830 us
  waiting for transfers between devices  1050 us (57%)
  matrix products  320 us (17%)
  local copies, waits for them, and re-layouts  211 us (11%)
  other arithmetic  93.8 us (5%)
  starting transfers between devices  81.8 us (4%)
  blocking collectives  39.8 us (2%)
    unnamed x24, waiting for transfers between devices  385 us
    reduce_scatter x1, waiting for transfers between devices, body(): lax.psum_scatter(terms.astype(jnp.bfloat16), 'blk', scatter_dimension=0,...  265 us
    ppermute x4, waiting for transfers between devices, body(): lower.append(lax.ppermute(lower[-1] if lower else mixed_low, 'blk', pairs))  139 us
    dynamic_slice x32, local copies, waits for them, and re-layouts, body(): lax.scan(inner_step, running, (key_piece.reshape(n_steps, step_rows, seq_...  74.7 us
    unnamed x109, local copies, waits for them, and re-layouts  74.2 us
    ppermute x3, starting transfers between devices, body(): upper.append(lax.ppermute(upper[-1] if upper else mixed_low, 'blk', back))  72.8 us
    reduce_scatter x1, waiting for transfers between devices, body(): lax.psum_scatter(weight_grads[4].astype(jnp.bfloat16), 'dp', scatter_dime...  55.1 us
    reduce_scatter x1, waiting for transfers between devices, body(): lax.psum_scatter(weight_grads[5].astype(jnp.bfloat16), 'dp', scatter_dime...  54.9 us
  transfers between devices with their start and end apart: 24, of which 19 were waited for; matrix products, arithmetic and copies ran while one was open for 20% of the time, Pallas kernels for 0%

profile of v1, /device:TPU:0, one launch (start us, length us, event | category | flops | bytes accessed | tf_op | source)
XLA Modules:
  0.0 1827.9 jit_solution(6879398368892517255)
XLA Ops:
  42.1 43.8 %collective-permute-done = bf16[256,2,1024]{2,0,1:T(8,128)(2,1)S(1)} collective-permute-done((bf16[256,2,1024]{2,0,1:T(8,128)(2,1)}, bf16[256,2,1024]{2,0,1:T(8,128)(2,1)S(1)}, u32[]{:S(2)}, u32[]{:S(2)}) %collective-permute-start) | collective-permute-done | bytes 1048608 | tf_op jit(solution)/shard_map/ppermute | solution.py:159
  91.7 55.0 %collective-permute-done.1 = bf16[256,2,1024]{2,0,1:T(8,128)(2,1)S(1)} collective-permute-done((bf16[256,2,1024]{2,0,1:T(8,128)(2,1)S(1)}, bf16[256,2,1024]{2,0,1:T(8,128)(2,1)S(1)}, u32[]{:S(2)}, u32[]{:S(2)}) %collective-permute-start.1) | collective-permute-done | bytes 1048608 | tf_op jit(solution)/shard_map/ppermute | solution.py:159
  150.0 45.4 %collective-permute-start.5 = (bf16[256,2,1024]{2,0,1:T(8,128)(2,1)}, bf16[256,2,1024]{2,0,1:T(8,128)(2,1)}, u32[]{:S(2)}, u32[]{:S(2)}) collective-permute-start(bf16[256,2,1024]{2,0,1:T(8,128)(2,1)} %collective-permute-done.4), channel_id=1, source_target_pairs={{1,0},{2,1},{3,2},{4,3},{5,4},{6,5},{7,6},{0,7},{9,8},{10,9},{11,1... | collective-permute-start | bytes 3145736 | tf_op jit(solution)/shard_map/ppermute | solution.py:161
  195.4 21.3 %collective-permute-done.2 = bf16[256,2,1024]{2,0,1:T(8,128)(2,1)} collective-permute-done((bf16[256,2,1024]{2,0,1:T(8,128)(2,1)S(1)}, bf16[256,2,1024]{2,0,1:T(8,128)(2,1)}, u32[]{:S(2)}, u32[]{:S(2)}) %collective-permute-start.2) | collective-permute-done | bytes 1048608 | tf_op jit(solution)/shard_map/ppermute | solution.py:159
  228.8 22.7 %collective-permute-start.6 = (bf16[256,2,1024]{2,0,1:T(8,128)(2,1)}, bf16[256,2,1024]{2,0,1:T(8,128)(2,1)S(1)}, u32[]{:S(2)}, u32[]{:S(2)}) collective-permute-start(bf16[256,2,1024]{2,0,1:T(8,128)(2,1)} %collective-permute-done.5), channel_id=1, source_target_pairs={{1,0},{2,1},{3,2},{4,3},{5,4},{6,5},{7,6},{0,7},{9,8},{10,9},{11,1... | collective-permute-start | bytes 3145736 | tf_op jit(solution)/shard_map/ppermute | solution.py:161
  251.5 19.0 %collective-permute-done.3 = bf16[256,2,1024]{2,0,1:T(8,128)(2,1)} collective-permute-done((bf16[256,2,1024]{2,0,1:T(8,128)(2,1)}, bf16[256,2,1024]{2,0,1:T(8,128)(2,1)}, u32[]{:S(2)}, u32[]{:S(2)}) %collective-permute-start.3) | collective-permute-done | bytes 1048608 | tf_op jit(solution)/shard_map/ppermute | solution.py:159
  300.1 11.6 copy.141
  311.7 165.6 %while.28 = (s32[]{:T(128)}, f32[2,16,256]{2,1,0:T(8,128)S(1)}, f32[2,16,256]{2,1,0:T(8,128)S(1)}, f32[2,16,256,64]{2,3,1,0:T(8,128)}, s32[4]{0:T(128)S(1)}, /*i...) while((s32[]{:T(128)}, f32[2,16,256]{2,1,0:T(8,128)S(1)}, ...), condition=%wide.region_7.8_spmd.clone, body=%wide.region_4.0_spmd.clone.sunk | while | flops 1122149120 | bytes 74207448 | solution.py:174
  341.4 11.9 fusion.163
  383.0 11.7 fusion.163
  424.3 11.7 fusion.163
  465.5 11.7 fusion.163
  519.2 212.7 %while.29 = (s32[]{:T(128)}, f32[256,2,16,64]{0,3,2,1:T(8,128)}, bf16[4,512,2,2048]{1,3,2,0:T(8,128)(2,1)}, bf16[4,512,2,1024]{1,3,2,0:T(8,128)(2,1)}, s32[4]{0:...) while((s32[]{:T(128)}, f32[256,2,16,64]{0,3,2,1:T(8,128)}, ...), condition=%wide.region_12.13_spmd.clone, body=%wide.region_11.12_spmd.clone.sunk | while | flops 2739012352 | bytes 133288232 | solution.py:267
  542.0 10.6 fusion.176
  593.9 10.6 fusion.176
  647.5 10.6 fusion.176
  732.0 22.1 %copy.150 = bf16[4,512,2,2048]{3,1,0,2:T(8,128)(2,1)} copy(bf16[4,512,2,2048]{1,3,2,0:T(8,128)(2,1)} %get-tuple-element.145) | data formatting | bytes 33554432 | tf_op jit(solution)/shard_map/convert_element_type | solution.py:278
  782.6 265.4 %reduce-scatter.30.cloned.1.call-done = bf16[256,2,2048]{2,0,1:T(8,128)(2,1)} async-done(((bf16[2048,2,2048]{2,0,1:T(8,128)(2,1)}), bf16[256,2,2048]{2,0,1:T(8,128)(2,1)}) %reduce-scatter.30.cloned.1.call-update) | async-done | bytes 2097168 | tf_op jit(solution)/shard_map/reduce_scatter | solution.py:277
  1055.2 26.4 %reduce-scatter.38.cloned.1.call-done = bf16[256,1024]{1,0:T(8,128)(2,1)} async-done(((bf16[1024,1024]{1,0:T(8,128)(2,1)}), bf16[256,1024]{1,0:T(8,128)(2,1)}) %reduce-scatter.38.cloned.1.call-update) | async-done | bytes 524304 | tf_op jit(solution)/shard_map/reduce_scatter | solution.py:309
  1083.7 55.1 %reduce-scatter.40.cloned.1.call-done = bf16[256,2816]{1,0:T(8,128)(2,1)} async-done(((bf16[1024,2816]{1,0:T(8,128)(2,1)}), bf16[256,2816]{1,0:T(8,128)(2,1)}) %reduce-scatter.40.cloned.1.call-update) | async-done | bytes 1441808 | tf_op jit(solution)/shard_map/reduce_scatter | solution.py:312
  1141.5 54.9 %reduce-scatter.42.cloned.1.call-done = bf16[256,2816]{1,0:T(8,128)(2,1)} async-done(((bf16[1024,2816]{1,0:T(8,128)(2,1)}), bf16[256,2816]{1,0:T(8,128)(2,1)}) %reduce-scatter.42.cloned.1.call-update) | async-done | bytes 1441808 | tf_op jit(solution)/shard_map/reduce_scatter | solution.py:315
  1199.0 54.8 %reduce-scatter.44.cloned.1.call-done = bf16[704,1024]{1,0:T(8,128)(2,1)} async-done(((bf16[2816,1024]{1,0:T(8,128)(2,1)}), bf16[704,1024]{1,0:T(8,128)(2,1)}) %reduce-scatter.44.cloned.1.call-update) | async-done | bytes 1441808 | tf_op jit(solution)/shard_map/reduce_scatter | solution.py:318
  1274.8 13.2 reduce-scatter.36.cloned.1.call-done
  1301.7 51.5 %reduce-scatter.52.cloned.1.call-done = bf16[128,256]{1,0:T(8,128)(2,1)} async-done(((bf16[1024,256]{1,0:T(8,128)(2,1)}), bf16[128,256]{1,0:T(8,128)(2,1)}) %reduce-scatter.52.cloned.1.call-update) | async-done | bytes 65552
  1354.9 66.0 %reduce-scatter.54.cloned.1.call-done = bf16[352,256]{1,0:T(8,128)(2,1)} async-done(((bf16[2816,256]{1,0:T(8,128)(2,1)}), bf16[352,256]{1,0:T(8,128)(2,1)}) %reduce-scatter.54.cloned.1.call-update) | async-done | bytes 180240
  1422.8 65.8 %reduce-scatter.56.cloned.1.call-done = bf16[352,256]{1,0:T(8,128)(2,1)} async-done(((bf16[2816,256]{1,0:T(8,128)(2,1)}), bf16[352,256]{1,0:T(8,128)(2,1)}) %reduce-scatter.56.cloned.1.call-update) | async-done | bytes 180240
  1490.6 65.4 %reduce-scatter.58.cloned.1.call-done = bf16[128,704]{1,0:T(8,128)(2,1)} async-done(((bf16[1024,704]{1,0:T(8,128)(2,1)}), bf16[128,704]{1,0:T(8,128)(2,1)}) %reduce-scatter.58.cloned.1.call-update) | async-done | bytes 180240
  1557.8 31.6 %reduce-scatter.34.cloned.1.call-done = bf16[256,1024]{1,0:T(8,128)(2,1)} async-done(((bf16[1024,1024]{1,0:T(8,128)(2,1)}), bf16[256,1024]{1,0:T(8,128)(2,1)}) %reduce-scatter.34.cloned.1.call-update) | async-done | bytes 524304 | tf_op jit(solution)/shard_map/reduce_scatter | solution.py:303
  1601.8 21.6 %reduce-scatter.32.cloned.1.call-done = bf16[256,1024]{1,0:T(8,128)(2,1)} async-done(((bf16[1024,1024]{1,0:T(8,128)(2,1)}), bf16[256,1024]{1,0:T(8,128)(2,1)}) %reduce-scatter.32.cloned.1.call-update) | async-done | bytes 524304 | tf_op jit(solution)/shard_map/reduce_scatter | solution.py:300
  1631.5 39.8 %all-reduce = (f32[1024]{0:T(1024)}, f32[1024]{0:T(1024)}, f32[]{:T(128)}, f32[]{:T(128)}) all-reduce(f32[1024]{0:T(1024)S(1)} %get-tuple-element.373, f32[1024]{0:T(1024)S(1)} %copy-done.36, f32[]{:T(128)} %fusion.47, f32[]{:T(128)} %get-tuple-element.444), channel_id=1, replica_groups=mesh['dp'=4,'blk'=8] {'dp','blk'}, use_global_device_ids=true, to_apply=%region_30.31 | all-reduce | flops 2050 | bytes 16400 | tf_op jit(solution)/shard_map/psum | solution.py:345
  1690.2 62.9 %reduce-scatter.48.cloned.1.call-done = bf16[128,256]{1,0:T(8,128)(2,1)} async-done(((bf16[1024,256]{1,0:T(8,128)(2,1)}), bf16[128,256]{1,0:T(8,128)(2,1)}) %reduce-scatter.48.cloned.1.call-update) | async-done | bytes 65552
  1754.7 62.5 %reduce-scatter.46.cloned.1.call-done = bf16[128,256]{1,0:T(8,128)(2,1)} async-done(((bf16[1024,256]{1,0:T(8,128)(2,1)}), bf16[128,256]{1,0:T(8,128)(2,1)}) %reduce-scatter.46.cloned.1.call-update) | async-done | bytes 65552
  (350 shorter events, 536.6 us)
Async XLA Ops:
  7.2 27.5 %copy-start = (bf16[1024,1024]{1,0:T(8,128)(2,1)S(1)}, bf16[1024,1024]{1,0:T(8,128)(2,1)}, u32[]{:S(2)}) copy-start(bf16[1024,1024]{1,0:T(8,128)(2,1)} %param.22) | copy-start | bytes 6291460
  7.2 292.9 %all-gather.3.cloned.1.call-start = ((), (), s32[]{:S(2)}) async-start(), calls=%async_computation.15 | async-start | bytes 9437184 | tf_op jit(solution)/shard_map/all_gather | solution.py:152
  9.8 24.8 %copy-start.33 = (f32[256,2]{0,1:T(2,128)}, f32[256,2]{0,1:T(2,128)S(1)}, u32[]{:S(2)}) copy-start(f32[256,2]{0,1:T(2,128)S(1)} %add_rsqrt_fusion.1) | copy-start | bytes 6148
  34.6 484.6 %all-gather.5.cloned.1.call-start = ((), (), s32[]{:S(2)}) async-start(), calls=%async_computation.16 | async-start | bytes 9437184 | tf_op jit(solution)/shard_map/all_gather | solution.py:219
  39.1 46.8 %collective-permute-start = (bf16[256,2,1024]{2,0,1:T(8,128)(2,1)}, bf16[256,2,1024]{2,0,1:T(8,128)(2,1)S(1)}, u32[]{:S(2)}, u32[]{:S(2)}) collective-permute-start(bf16[256,2,1024]{2,0,1:T(8,128)(2,1)} %get-tuple-element.445), channel_id=1, source_target_pairs={{0,1},{1,2},{2,3},{3,4},{4,5},{5,6},{6,7},{7,0},{8,9},{9,10},{10,1... | collective-permute-start | bytes 3145736 | tf_op jit(solution)/shard_map/ppermute | solution.py:159
  86.9 59.8 %collective-permute-start.1 = (bf16[256,2,1024]{2,0,1:T(8,128)(2,1)S(1)}, bf16[256,2,1024]{2,0,1:T(8,128)(2,1)S(1)}, u32[]{:S(2)}, u32[]{:S(2)}) collective-permute-start(bf16[256,2,1024]{2,0,1:T(8,128)(2,1)S(1)} %collective-permute-done), channel_id=1, source_target_pairs={{0,1},{1,2},{2,3},{3,4},{4,5},{5,6},{6,7},{7,0},{8,9},{9,10},{10,1... | collective-permute-start | bytes 3145736 | tf_op jit(solution)/shard_map/ppermute | solution.py:159
  86.9 63.0 %collective-permute-start.4 = (bf16[256,2,1024]{2,0,1:T(8,128)(2,1)}, bf16[256,2,1024]{2,0,1:T(8,128)(2,1)}, u32[]{:S(2)}, u32[]{:S(2)}) collective-permute-start(bf16[256,2,1024]{2,0,1:T(8,128)(2,1)} %get-tuple-element.445), channel_id=1, source_target_pairs={{1,0},{2,1},{3,2},{4,3},{5,4},{6,5},{7,6},{0,7},{9,8},{10,9},{11,1... | collective-permute-start | bytes 3145736 | tf_op jit(solution)/shard_map/ppermute | solution.py:161
  146.7 72.6 %copy-start.20 = (bf16[256,2,1024]{2,0,1:T(8,128)(2,1)}, bf16[256,2,1024]{2,0,1:T(8,128)(2,1)S(1)}, u32[]{:S(2)}) copy-start(bf16[256,2,1024]{2,0,1:T(8,128)(2,1)S(1)} %collective-permute-done.1) | copy-start | bytes 3145732
  146.7 69.9 %collective-permute-start.2 = (bf16[256,2,1024]{2,0,1:T(8,128)(2,1)S(1)}, bf16[256,2,1024]{2,0,1:T(8,128)(2,1)}, u32[]{:S(2)}, u32[]{:S(2)}) collective-permute-start(bf16[256,2,1024]{2,0,1:T(8,128)(2,1)S(1)} %collective-permute-done.1), channel_id=1, source_target_pairs={{0,1},{1,2},{2,3},{3,4},{4,5},{5,6},{6,7},{7,0},{8,9},{9,10},{10,1... | collective-permute-start | bytes 3145736 | tf_op jit(solution)/shard_map/ppermute | solution.py:159
  149.2 898.8 %reduce-scatter.30.cloned.1.call-start = ((), (), s32[]{:S(2)}) async-start(), calls=%async_computation.17 | async-start | bytes 18874368 | tf_op jit(solution)/shard_map/reduce_scatter | solution.py:277
  150.0 78.8 %collective-permute-start.5 = (bf16[256,2,1024]{2,0,1:T(8,128)(2,1)}, bf16[256,2,1024]{2,0,1:T(8,128)(2,1)}, u32[]{:S(2)}, u32[]{:S(2)}) collective-permute-start(bf16[256,2,1024]{2,0,1:T(8,128)(2,1)} %collective-permute-done.4), channel_id=1, source_target_pairs={{1,0},{2,1},{3,2},{4,3},{5,4},{6,5},{7,6},{0,7},{9,8},{10,9},{11,1... | collective-permute-start | bytes 3145736 | tf_op jit(solution)/shard_map/ppermute | solution.py:161
  216.6 53.9 %collective-permute-start.3 = (bf16[256,2,1024]{2,0,1:T(8,128)(2,1)}, bf16[256,2,1024]{2,0,1:T(8,128)(2,1)}, u32[]{:S(2)}, u32[]{:S(2)}) collective-permute-start(bf16[256,2,1024]{2,0,1:T(8,128)(2,1)} %collective-permute-done.2), channel_id=1, source_target_pairs={{0,1},{1,2},{2,3},{3,4},{4,5},{5,6},{6,7},{7,0},{8,9},{9,10},{10,1... | collective-permute-start | bytes 3145736 | tf_op jit(solution)/shard_map/ppermute | solution.py:159
  228.8 46.5 %copy-start.21 = (bf16[256,2,1024]{2,0,1:T(8,128)(2,1)S(1)}, bf16[256,2,1024]{2,0,1:T(8,128)(2,1)}, u32[]{:S(2)}) copy-start(bf16[256,2,1024]{2,0,1:T(8,128)(2,1)} %copy-done.20) | copy-start | bytes 3145732
  228.8 54.2 %collective-permute-start.6 = (bf16[256,2,1024]{2,0,1:T(8,128)(2,1)}, bf16[256,2,1024]{2,0,1:T(8,128)(2,1)S(1)}, u32[]{:S(2)}, u32[]{:S(2)}) collective-permute-start(bf16[256,2,1024]{2,0,1:T(8,128)(2,1)} %collective-permute-done.5), channel_id=1, source_target_pairs={{1,0},{2,1},{3,2},{4,3},{5,4},{6,5},{7,6},{0,7},{9,8},{10,9},{11,1... | collective-permute-start | bytes 3145736 | tf_op jit(solution)/shard_map/ppermute | solution.py:161
  481.3 29.1 %copy-start.3 = (f32[256,2,1024]{2,0,1:T(8,128)}, f32[256,2,1024]{2,0,1:T(8,128)S(1)}, u32[]{:S(2)}) copy-start(f32[256,2,1024]{2,0,1:T(8,128)S(1)} %get-tuple-element.455) | copy-start | bytes 6291460
  754.1 327.5 %reduce-scatter.38.cloned.1.call-start = ((), (), s32[]{:S(2)}) async-start(), calls=%async_computation.21 | async-start | bytes 2621440 | tf_op jit(solution)/shard_map/reduce_scatter | solution.py:309
  759.5 379.4 %reduce-scatter.40.cloned.1.call-start = ((), (), s32[]{:S(2)}) async-start(), calls=%async_computation.22 | async-start | bytes 7208960 | tf_op jit(solution)/shard_map/reduce_scatter | solution.py:312
  767.5 428.9 %reduce-scatter.42.cloned.1.call-start = ((), (), s32[]{:S(2)}) async-start(), calls=%async_computation.23 | async-start | bytes 7208960 | tf_op jit(solution)/shard_map/reduce_scatter | solution.py:315
  774.3 479.5 %reduce-scatter.44.cloned.1.call-start = ((), (), s32[]{:S(2)}) async-start(), calls=%async_computation.24 | async-start | bytes 7208960 | tf_op jit(solution)/shard_map/reduce_scatter | solution.py:318
  782.5 269.6 %copy-start.7 = (bf16[256,2,1024]{2,1,0:T(2,128)(2,1)S(1)}, bf16[256,2,1024]{2,1,0:T(2,128)(2,1)}, u32[]{:S(2)}) copy-start(bf16[256,2,1024]{2,1,0:T(2,128)(2,1)} %param.17) | copy-start | bytes 3145732
  782.5 269.6 %copy-start.32 = (f32[1024]{0:T(1024)S(1)}, f32[1024]{0:T(1024)}, u32[]{:S(2)}) copy-start(f32[1024]{0:T(1024)} %param.27) | copy-start | bytes 12292
  782.5 269.5 %copy-start.34 = (f32[256,2]{0,1:T(2,128)S(1)}, f32[256,2]{0,1:T(2,128)}, u32[]{:S(2)}) copy-start(f32[256,2]{0,1:T(2,128)} %copy-done.33) | copy-start | bytes 6148
  782.5 505.4 %reduce-scatter.36.cloned.1.call-start = ((), (), s32[]{:S(2)}) async-start(), calls=%async_computation.20 | async-start | bytes 2621440 | tf_op jit(solution)/shard_map/reduce_scatter | solution.py:306
  1055.1 298.1 %reduce-scatter.52.cloned.1.call-start = ((), (), s32[]{:S(2)}) async-start(), calls=%async_computation.28 | async-start | bytes 589824
  1083.7 337.2 %reduce-scatter.54.cloned.1.call-start = ((), (), s32[]{:S(2)}) async-start(), calls=%async_computation.29 | async-start | bytes 1622016
  1141.5 347.2 %reduce-scatter.56.cloned.1.call-start = ((), (), s32[]{:S(2)}) async-start(), calls=%async_computation.30 | async-start | bytes 1622016
  1198.9 357.1 %reduce-scatter.58.cloned.1.call-start = ((), (), s32[]{:S(2)}) async-start(), calls=%async_computation.31 | async-start | bytes 1769472
  1256.4 333.0 %reduce-scatter.34.cloned.1.call-start = ((), (), s32[]{:S(2)}) async-start(), calls=%async_computation.19 | async-start | bytes 2621440 | tf_op jit(solution)/shard_map/reduce_scatter | solution.py:303
  1270.6 352.8 %reduce-scatter.32.cloned.1.call-start = ((), (), s32[]{:S(2)}) async-start(), calls=%async_computation.18 | async-start | bytes 2621440 | tf_op jit(solution)/shard_map/reduce_scatter | solution.py:300
  1274.7 413.9 %reduce-scatter.50.cloned.1.call-start = ((), (), s32[]{:S(2)}) async-start(), calls=%async_computation.27 | async-start | bytes 589824
  1290.0 463.1 %reduce-scatter.48.cloned.1.call-start = ((), (), s32[]{:S(2)}) async-start(), calls=%async_computation.26 | async-start | bytes 589824
  1591.5 225.7 %reduce-scatter.46.cloned.1.call-start = ((), (), s32[]{:S(2)}) async-start(), calls=%async_computation.25 | async-start | bytes 589824
  (40 other events, 173.2 us)
Sparse Core Ops, SparseCore 0:
  34.8 239.4 all-gather.2
  277.1 143.0 all-gather.4
  754.2 293.7 reduce-scatter.29
  1051.1 30.4 reduce-scatter.37
  1084.0 54.8 reduce-scatter.39
  1141.4 54.8 reduce-scatter.41
  1198.9 54.8 reduce-scatter.43
  1256.5 31.3 reduce-scatter.35
  1291.3 61.8 reduce-scatter.51
  1356.9 63.9 reduce-scatter.53
  1424.6 63.9 reduce-scatter.55
  1492.3 63.6 reduce-scatter.57
  1559.1 30.2 reduce-scatter.33
  1591.9 31.4 reduce-scatter.31
  1626.6 61.9 reduce-scatter.49
  1692.2 60.8 reduce-scatter.47
  1756.3 60.8 reduce-scatter.45
